TPU v7x, 32 devices: a whole 2x2x4 slice. The times are simulated.
32 devices in a mesh: enc: 2 (over core), dp: 4 (over z), mp: 4 (over y, x).
Axes of the slice: x: 2, y: 2, z: 4, core: 2. Of those that a mesh axis runs over, the one named last changes fastest.
Arguments:
- token_ids: int32 [2, 16, 256], P('enc', 'dp'), may hold values from 0 to 30719
- query_lengths: int32 [32], P('dp'), may hold values from 1 to 128, 2048 in all
- negative_mask: int32 [32, 16], replicated, may hold values 0 or 1
- positive_index: int32 [32], replicated, may hold values from 0 to 15
- used_rows: int32 [32], replicated, may hold values 0 or 1
- step_count: int32 [1], replicated, may hold values from 2 to 20
- table: float32 [2, 30720, 768], P('enc', ('dp', 'mp')), may hold values from -0.18 to 0.18
- w_mixed: float32 [2, 768, 3, 768], P('enc', 'dp', None, 'mp'), may hold values from -0.21875 to 0.21875
- w_out: float32 [2, 768, 768], P('enc', 'mp', 'dp'), may hold values from -0.875 to 0.875
- w_inner: float32 [2, 768, 3072], P('enc', 'dp', 'mp'), may hold values from -0.21875 to 0.21875
- w_outer: float32 [2, 3072, 768], P('enc', 'mp', 'dp'), may hold values from -0.109375 to 0.109375
- norm_params: float32 [2, 6, 768], P('enc'), as said below
- table_m: float32 [2, 30720, 768], P('enc', ('dp', 'mp')), may hold values from -1.1234977e-06 to 1.1234977e-06
- table_v: float32 [2, 30720, 768], P('enc', ('dp', 'mp')), may hold values from 6.5198705e-15 to 2.6079482e-14
- mixed_m: float32 [2, 768, 3, 768], P('enc', 'dp', None, 'mp'), may hold values from -1.1234977e-06 to 1.1234977e-06
- mixed_v: float32 [2, 768, 3, 768], P('enc', 'dp', None, 'mp'), may hold values from 6.5198705e-15 to 2.6079482e-14
- out_m: float32 [2, 768, 768], P('enc', 'mp', 'dp'), may hold values from -1.1234977e-06 to 1.1234977e-06
- out_v: float32 [2, 768, 768], P('enc', 'mp', 'dp'), may hold values from 6.5198705e-15 to 2.6079482e-14
- inner_m: float32 [2, 768, 3072], P('enc', 'dp', 'mp'), may hold values from -1.1234977e-06 to 1.1234977e-06
- inner_v: float32 [2, 768, 3072], P('enc', 'dp', 'mp'), may hold values from 6.5198705e-15 to 2.6079482e-14
- outer_m: float32 [2, 3072, 768], P('enc', 'mp', 'dp'), may hold values from -1.1234977e-06 to 1.1234977e-06
- outer_v: float32 [2, 3072, 768], P('enc', 'mp', 'dp'), may hold values from 6.5198705e-15 to 2.6079482e-14
- norms_m: float32 [2, 6, 768], P('enc'), may hold values from -4.4684566e-06 to 4.4684566e-06
- norms_v: float32 [2, 6, 768], P('enc'), may hold values from 1.0431793e-13 to 4.172717e-13
Outputs:
- loss: float32 [], replicated
- grad_norm: float32 [], replicated
- table_new: float32 [2, 30720, 768], P('enc', ('dp', 'mp'))
- table_m_new: float32 [2, 30720, 768], P('enc', ('dp', 'mp'))
- table_v_new: float32 [2, 30720, 768], P('enc', ('dp', 'mp'))
- mixed_new: float32 [2, 768, 3, 768], P('enc', 'dp', None, 'mp')
- mixed_m_new: float32 [2, 768, 3, 768], P('enc', 'dp', None, 'mp')
- mixed_v_new: float32 [2, 768, 3, 768], P('enc', 'dp', None, 'mp')
- out_new: float32 [2, 768, 768], P('enc', 'mp', 'dp')
- out_m_new: float32 [2, 768, 768], P('enc', 'mp', 'dp')
- output_second_moment_next: float32 [2, 768, 768], P('enc', 'mp', 'dp')
- inner_new: float32 [2, 768, 3072], P('enc', 'dp', 'mp')
- inner_m_new: float32 [2, 768, 3072], P('enc', 'dp', 'mp')
- inner_v_new: float32 [2, 768, 3072], P('enc', 'dp', 'mp')
- outer_new: float32 [2, 3072, 768], P('enc', 'mp', 'dp')
- outer_m_new: float32 [2, 3072, 768], P('enc', 'mp', 'dp')
- outer_v_new: float32 [2, 3072, 768], P('enc', 'mp', 'dp')
- norms_new: float32 [2, 6, 768], P('enc')
- norms_m_new: float32 [2, 6, 768], P('enc')
- norms_v_new: float32 [2, 6, 768], P('enc')
Inputs may be any that keep to these rules, and one draw needn't show every extreme that they name: `norm_params`: gains (rows 0, 2, 4) lie in 0.7 to 1.3, shifts (rows 1, 3, 5) are small.
All inputs are finite; a program needn't handle non-finite values. No bound on the sum of `query_lengths` on one device may be relied on, other than what follows from the above.
Results may differ from a plain program's by a relative error of at most 0.015.
Values may be sent and summed in bfloat16 or wider, within the bound.
A program may use at most 192 MiB of HBM per device.

v0:
```python
from functools import partial
import jax
import jax.numpy as jnp
from jax import lax
from jax.sharding import PartitionSpec as P

D = 768
HEAD = 64
QSLOT = 128
SPANS = 2
exact_arithmetic_level = lax.Precision.HIGHEST
eps_norm = 1e-06
logit_divisor = 0.05
clip_limit = 0.02
beta_one = 0.9
beta_two = 0.999
adam_eps = 1e-08


def layer_norm(x, gain, shift):
    centred = x - jnp.mean(x, -1, keepdims=True)
    spread = jnp.mean(centred * centred, -1, keepdims=True)
    return centred * lax.rsqrt(spread + eps_norm) * gain + shift


def spread_rows(x):
    return lax.all_gather(x, "mp", axis=0, tiled=True)


def collect_rows(x):
    return lax.psum_scatter(x, "mp", scatter_dimension=0, tiled=True)


def contract_rows(left, right):
    return lax.dot_general(
        left, right, (((0,), (0,)), ((), ())), preferred_element_type=jnp.float32
    )


def contract_cols(left, right):
    return lax.dot_general(
        left, right, (((1,), (1,)), ((), ())), preferred_element_type=jnp.float32
    )


def vocab_place(flat_ids, table_rows):
    n_mp = lax.axis_size("mp")
    piece = table_rows // lax.axis_size("dp")
    block_num = flat_ids // piece
    local_row = block_num // n_mp * piece + flat_ids % piece
    owned = block_num % n_mp == lax.axis_index("mp")
    return (local_row, owned)


def attention_mask(lens_span, is_query, length):
    diagonal_indices = jnp.arange(length)
    segment = jnp.where(is_query, diagonal_indices // QSLOT, 0)
    limit = jnp.where(diagonal_indices[None, :] < QSLOT, lens_span[:, 0:1], lens_span[:, 1:2])
    key_ok = jnp.where(is_query, (diagonal_indices % QSLOT)[None, :] < limit, True)
    return (segment[:, None] == segment[None, :])[None] & key_ok[:, None, :]


def attention_scores(queries, keys, allowed):
    scores = jnp.einsum(
        "bqhd,bkhd->bhqk", queries, keys, preferred_element_type=jnp.float32
    ) * HEAD ** (-0.5)
    return jnp.where(allowed[:, None], scores, -1e30)


def forward_span(weights, norms, ids_span, allowed):
    table, w_mixed, w_out, w_inner, w_outer = weights
    blocks, length = ids_span.shape
    rows = blocks * length
    local_row, owned = vocab_place(ids_span.reshape(rows), table.shape[0])
    looked = jnp.where(owned[:, None], table[local_row].astype(jnp.float32), 0.0)
    embedded = lax.psum_scatter(
        looked.astype(jnp.bfloat16), "mp", scatter_dimension=0, tiled=True
    ).astype(jnp.float32)
    hidden0 = layer_norm(embedded, norms[0], norms[1])
    hid_all = spread_rows(hidden0.astype(jnp.bfloat16))
    mixed = jnp.dot(hid_all, w_mixed.reshape(D, -1), preferred_element_type=jnp.float32).astype(
        jnp.bfloat16
    )
    heads_local = w_out.shape[0] // HEAD
    parts = mixed.reshape(blocks, length, 3, heads_local, HEAD)
    scores = attention_scores(parts[:, :, 0], parts[:, :, 1], allowed)
    top = jnp.max(scores, -1, keepdims=True)
    log_total = top + jnp.log(jnp.sum(jnp.exp(scores - top), -1, keepdims=True))
    probs = jnp.exp(scores - log_total).astype(jnp.bfloat16)
    attended = jnp.einsum(
        "bhqk,bkhd->bqhd", probs, parts[:, :, 2], preferred_element_type=jnp.float32
    )
    attended = attended.astype(jnp.bfloat16).reshape(rows, -1)
    first_sum = hidden0 + collect_rows(jnp.dot(attended, w_out, preferred_element_type=jnp.float32))
    normed = layer_norm(first_sum, norms[2], norms[3])
    rescaled_everything = spread_rows(normed.astype(jnp.bfloat16))
    inner = jnp.dot(rescaled_everything, w_inner, preferred_element_type=jnp.float32)
    activated = jax.nn.gelu(inner, approximate=False).astype(jnp.bfloat16)
    second_sum = normed + collect_rows(
        jnp.dot(activated, w_outer, preferred_element_type=jnp.float32)
    )
    final = layer_norm(second_sum, norms[4], norms[5])
    saved = (
        embedded,
        hid_all,
        parts,
        log_total,
        attended,
        first_sum,
        rescaled_everything,
        inner,
        activated,
        second_sum,
    )
    return (final, saved)


def backward_span(weights, norms, ids_span, allowed, saved, grad_final):
    table, w_mixed, w_out, w_inner, w_outer = weights
    (
        embedded,
        hid_all,
        parts,
        log_total,
        attended,
        first_sum,
        rescaled_everything,
        inner,
        activated,
        second_sum,
    ) = saved
    blocks, length = ids_span.shape
    rows = blocks * length
    _, length_scaling_pullback = jax.vjp(layer_norm, second_sum, norms[4], norms[5])
    d_second, d_gain2, d_shift2 = length_scaling_pullback(grad_final)
    d_outer = spread_rows(d_second.astype(jnp.bfloat16))
    g_outer = contract_rows(activated, d_outer)
    d_act = contract_cols(d_outer, w_outer)
    _, gelu_back = jax.vjp(partial(jax.nn.gelu, approximate=False), inner)
    d_inner = gelu_back(d_act)[0].astype(jnp.bfloat16)
    g_inner = contract_rows(rescaled_everything, d_inner)
    d_normed = d_second + collect_rows(contract_cols(d_inner, w_inner))
    _, length_scaling_pullback = jax.vjp(layer_norm, first_sum, norms[2], norms[3])
    d_first, d_gain1, shift_gradient_middle = length_scaling_pullback(d_normed)
    d_attn = spread_rows(d_first.astype(jnp.bfloat16))
    g_out = contract_rows(attended, d_attn)
    d_attended = contract_cols(d_attn, w_out).astype(jnp.bfloat16).reshape(blocks, length, -1, HEAD)
    queries, keys, values = (parts[:, :, 0], parts[:, :, 1], parts[:, :, 2])
    probs = jnp.exp(attention_scores(queries, keys, allowed) - log_total)
    d_values = jnp.einsum(
        "bhqk,bqhd->bkhd",
        probs.astype(jnp.bfloat16),
        d_attended,
        preferred_element_type=jnp.float32,
    )
    d_probs = jnp.einsum("bqhd,bkhd->bhqk", d_attended, values, preferred_element_type=jnp.float32)
    d_scores = (probs * (d_probs - jnp.sum(probs * d_probs, -1, keepdims=True))).astype(
        jnp.bfloat16
    )
    d_queries = jnp.einsum(
        "bhqk,bkhd->bqhd", d_scores, keys, preferred_element_type=jnp.float32
    ) * HEAD ** (-0.5)
    d_keys = jnp.einsum(
        "bhqk,bqhd->bkhd", d_scores, queries, preferred_element_type=jnp.float32
    ) * HEAD ** (-0.5)
    d_mixed = jnp.stack([d_queries, d_keys, d_values], 2).astype(jnp.bfloat16).reshape(rows, -1)
    g_mixed = contract_rows(hid_all, d_mixed).reshape(w_mixed.shape)
    d_hidden = d_first + collect_rows(contract_cols(d_mixed, w_mixed.reshape(D, -1)))
    _, length_scaling_pullback = jax.vjp(layer_norm, embedded, norms[0], norms[1])
    d_embedded, d_gain0, d_shift0 = length_scaling_pullback(d_hidden)
    g_norms = jnp.stack([d_gain0, d_shift0, d_gain1, shift_gradient_middle, d_gain2, d_shift2])
    return ((g_mixed, g_out, g_inner, g_outer), d_embedded, g_norms)


def cls_picker(blocks, length):
    n_mp = lax.axis_size("mp")
    shard = blocks * length // n_mp
    global_row = lax.axis_index("mp") * shard + jnp.arange(shard)
    within = global_row % length
    slot = global_row // length * 2 + within // QSLOT
    hits = (slot[None, :] == jnp.arange(2 * blocks)[:, None]) & (within % QSLOT == 0)[None, :]
    return hits.astype(jnp.float32)


def contrast(queries, passages, negative_mask, positive_index, used_rows):
    question_direction_rows = queries * lax.rsqrt(
        jnp.sum(queries * queries, -1, keepdims=True) + eps_norm
    )
    document_direction_rows = passages * lax.rsqrt(
        jnp.sum(passages * passages, -1, keepdims=True) + eps_norm
    )
    pairwise_cosine_table = (
        jnp.dot(
            question_direction_rows, document_direction_rows.T, precision=exact_arithmetic_level
        )
        / logit_divisor
    )
    excluded = (negative_mask == 1) & (
        jnp.arange(passages.shape[0])[None, :] != positive_index[:, None]
    )
    pairwise_cosine_table = jnp.where(excluded, -1e30, pairwise_cosine_table)
    top = jnp.max(pairwise_cosine_table, -1, keepdims=True)
    log_total = top[:, 0] + jnp.log(jnp.sum(jnp.exp(pairwise_cosine_table - top), -1))
    target = jnp.take_along_axis(pairwise_cosine_table, positive_index[:, None], 1)[:, 0]
    weight = used_rows.astype(jnp.float32)
    return jnp.sum(weight * (log_total - target)) / jnp.maximum(jnp.sum(weight), 1.0)


def adam_step(weight, grad, first, second, rate, decay, count):
    first_new = beta_one * first + (1.0 - beta_one) * grad
    second_new = beta_two * second + (1.0 - beta_two) * grad * grad
    fix_one = 1.0 - jnp.power(beta_one, count)
    correction_second = 1.0 - jnp.power(beta_two, count)
    update = (
        first_new / fix_one / (jnp.sqrt(second_new / correction_second) + adam_eps) + decay * weight
    )
    return (weight - rate * update, first_new, second_new)


def on_device(
    token_ids,
    query_lengths,
    negative_mask,
    positive_index,
    used_rows,
    step_count,
    table,
    w_mixed,
    w_out,
    w_inner,
    w_outer,
    norm_params,
    table_m,
    table_v,
    mixed_m,
    mixed_v,
    out_m,
    out_v,
    inner_m,
    inner_v,
    outer_m,
    outer_v,
    norms_m,
    norms_v,
):
    is_query = lax.axis_index("enc") == 0
    gathered = (
        lax.all_gather(table.astype(jnp.bfloat16), "dp", axis=1, tiled=True),
        lax.all_gather(w_mixed.astype(jnp.bfloat16), "dp", axis=1, tiled=True),
        lax.all_gather(w_out.astype(jnp.bfloat16), "dp", axis=2, tiled=True),
        lax.all_gather(w_inner.astype(jnp.bfloat16), "dp", axis=1, tiled=True),
        lax.all_gather(w_outer.astype(jnp.bfloat16), "dp", axis=2, tiled=True),
    )
    weights = tuple((item[0] for item in gathered))
    norms = norm_params[0]
    ids_all = token_ids[0]
    blk, length = ids_all.shape
    per_span = blk // SPANS
    lens_all = query_lengths.reshape(blk, 2)
    picker = cls_picker(per_span, length)
    masks, saved_list, cls_parts = ([], [], [])
    for index in range(SPANS):
        ids_span = ids_all[index * per_span : (index + 1) * per_span]
        allowed = attention_mask(
            lens_all[index * per_span : (index + 1) * per_span], is_query, length
        )
        final, saved = forward_span(weights, norms, ids_span, allowed)
        cls_parts.append(jnp.dot(picker, final, precision=exact_arithmetic_level))
        masks.append(allowed)
        saved_list.append(saved)
    cls_mine = lax.psum(jnp.concatenate(cls_parts, 0), "mp")
    cls_all = lax.all_gather(cls_mine, ("enc", "dp"), axis=0, tiled=True)
    n_dp = lax.axis_size("dp")
    cls_all = cls_all.reshape(2, n_dp * 2 * blk, D)
    queries = cls_all[0]
    passages = cls_all[1, 0::2]
    loss, loss_back = jax.vjp(
        partial(
            contrast,
            negative_mask=negative_mask,
            positive_index=positive_index,
            used_rows=used_rows,
        ),
        queries,
        passages,
    )
    d_queries, d_passages = loss_back(jnp.ones((), jnp.float32))
    d_pass_full = jnp.zeros_like(queries).at[0::2].set(d_passages)
    d_cls = jnp.where(is_query, d_queries, d_pass_full)
    d_mine = lax.dynamic_slice_in_dim(d_cls, lax.axis_index("dp") * 2 * blk, 2 * blk, 0)
    totals = None
    g_norms = jnp.zeros((6, D), jnp.float32)
    for index in range(SPANS):
        ids_span = ids_all[index * per_span : (index + 1) * per_span]
        _, saved = forward_span(weights, norms, ids_span, masks[index])
        grad_final = lax.dot_general(
            picker,
            d_mine[index * 2 * per_span : (index + 1) * 2 * per_span],
            (((0,), (0,)), ((), ())),
            precision=exact_arithmetic_level,
            preferred_element_type=jnp.float32,
        )
        mats, d_embedded, span_norms = backward_span(
            weights, norms, ids_span, masks[index], saved, grad_final
        )
        g_norms = g_norms + span_norms
        flat_ids = ids_span.reshape(-1)
        d_rows = lax.all_gather(d_embedded, "mp", axis=0, tiled=True)
        local_row, owned = vocab_place(flat_ids, weights[0].shape[0])
        g_table = (
            jnp.zeros(weights[0].shape, jnp.float32)
            .at[local_row]
            .add(jnp.where(owned[:, None], d_rows, 0.0))
        )
        span_grads = (g_table,) + mats
        totals = (
            span_grads if totals is None else tuple((a + b for a, b in zip(totals, span_grads)))
        )
    shards = (
        lax.psum_scatter(totals[0][None], "dp", scatter_dimension=1, tiled=True),
        lax.psum_scatter(totals[1][None], "dp", scatter_dimension=1, tiled=True),
        lax.psum_scatter(totals[2][None], "dp", scatter_dimension=2, tiled=True),
        lax.psum_scatter(totals[3][None], "dp", scatter_dimension=1, tiled=True),
        lax.psum_scatter(totals[4][None], "dp", scatter_dimension=2, tiled=True),
    )
    g_norms = lax.psum(g_norms, ("dp", "mp"))
    owner = (lax.axis_index("dp") == 0) & (lax.axis_index("mp") == 0)
    squares = jnp.where(owner, jnp.sum(g_norms * g_norms), 0.0)
    for shard in shards:
        squares = squares + jnp.sum(shard * shard)
    grad_norm = jnp.sqrt(lax.psum(squares, ("enc", "dp", "mp")))
    clip = jnp.minimum(1.0, clip_limit / (grad_norm + 1e-06))
    count = step_count[0].astype(jnp.float32)
    masters = (table, w_mixed, w_out, w_inner, w_outer)
    firsts = (table_m, mixed_m, out_m, inner_m, outer_m)
    seconds = (table_v, mixed_v, out_v, inner_v, outer_v)
    results = []
    for index in range(5):
        results.append(
            adam_step(
                masters[index],
                shards[index] * clip,
                firsts[index],
                seconds[index],
                0.06,
                0.01,
                count,
            )
        )
    results.append(adam_step(norm_params, g_norms[None] * clip, norms_m, norms_v, 0.5, 0.0, count))
    return (
        loss,
        grad_norm,
        results[0][0],
        results[0][1],
        results[0][2],
        results[1][0],
        results[1][1],
        results[1][2],
        results[2][0],
        results[2][1],
        results[2][2],
        results[3][0],
        results[3][1],
        results[3][2],
        results[4][0],
        results[4][1],
        results[4][2],
        results[5][0],
        results[5][1],
        results[5][2],
    )


def solution(mesh):
    placed = (
        P("enc", "dp", None),
        P("dp"),
        P(),
        P(),
        P(),
        P(),
        P("enc", ("dp", "mp"), None),
        P("enc", "dp", None, "mp"),
        P("enc", "mp", "dp"),
        P("enc", "dp", "mp"),
        P("enc", "mp", "dp"),
        P("enc", None, None),
        P("enc", ("dp", "mp"), None),
        P("enc", ("dp", "mp"), None),
        P("enc", "dp", None, "mp"),
        P("enc", "dp", None, "mp"),
        P("enc", "mp", "dp"),
        P("enc", "mp", "dp"),
        P("enc", "dp", "mp"),
        P("enc", "dp", "mp"),
        P("enc", "mp", "dp"),
        P("enc", "mp", "dp"),
        P("enc", None, None),
        P("enc", None, None),
    )
    return jax.shard_map(
        on_device,
        mesh=mesh,
        in_specs=placed,
        out_specs=(
            P(),
            P(),
            P("enc", ("dp", "mp"), None),
            P("enc", ("dp", "mp"), None),
            P("enc", ("dp", "mp"), None),
            P("enc", "dp", None, "mp"),
            P("enc", "dp", None, "mp"),
            P("enc", "dp", None, "mp"),
            P("enc", "mp", "dp"),
            P("enc", "mp", "dp"),
            P("enc", "mp", "dp"),
            P("enc", "dp", "mp"),
            P("enc", "dp", "mp"),
            P("enc", "dp", "mp"),
            P("enc", "mp", "dp"),
            P("enc", "mp", "dp"),
            P("enc", "mp", "dp"),
            P("enc", None, None),
            P("enc", None, None),
            P("enc", None, None),
        ),
        check_vma=False,
    )
```

profile of v0, /device:TPU:0, one launch (start us, length us, event | category | flops | bytes accessed | tf_op | source)
XLA Modules:
  0.0 1548.0 jit_solution(6013270489068151891)
XLA Ops:
  7.2 4.6 convert_element_type.165
  13.2 50.5 %all_gather.54 = bf16[1,768,3,192]{3,2,0,1:T(4,128)(2,1)S(1)} all-gather(bf16[1,192,3,192]{3,2,0,1:T(4,128)(2,1)S(1)} %copy.212), channel_id=1, replica_groups=mesh['enc'=2,'dp'=4,'mp'=4] {'dp'}, dimensions={1}, use_global_device_ids=true | all-gather | bytes 1105920 | tf_op jit(solution)/shard_map/all_gather | solution.py:249
  65.0 32.1 %all_gather.55 = bf16[1,192,768]{1,0,2:T(2,128)(2,1)S(1)} all-gather(bf16[1,192,192]{1,0,2:T(2,128)(2,1)S(1)} %copy.219), channel_id=1, replica_groups=mesh['enc'=2,'dp'=4,'mp'=4] {'dp'}, dimensions={2}, use_global_device_ids=true | all-gather | bytes 368640 | tf_op jit(solution)/shard_map/all_gather | solution.py:250
  97.7 150.2 %all-gather.6.cloned.1.call-done = bf16[1,7680,768]{2,1,0:T(8,128)(2,1)} async-done(((bf16[1,1920,768]{2,1,0:T(8,128)(2,1)}), bf16[1,7680,768]{2,1,0:T(8,128)(2,1)}) %all-gather.6.cloned.1.call-update) | async-done | bytes 11796496 | tf_op jit(solution)/shard_map/all_gather | solution.py:248
  248.0 8.3 gather_fusion
  259.4 8.4 gather_fusion.1
  268.9 14.0 reduce-scatter.19.cloned.1.call-done
  286.3 14.5 all_gather.53
  309.4 4.0 reduce-scatter.25.cloned.1.call-done
  316.2 31.6 %reduce-scatter.21.cloned.1.call-done = f32[128,768]{1,0:T(8,128)} async-done(((f32[512,768]{1,0:T(8,128)}), f32[128,768]{1,0:T(8,128)}) %reduce-scatter.21.cloned.1.call-update) | async-done | bytes 393232 | tf_op jit(solution)/shard_map/reduce_scatter | solution.py:31
  349.6 11.3 all_gather.59
  372.4 11.2 all_gather.56
  383.6 7.2 multiply_convert_fusion.3
  390.9 20.9 %all-gather.10.cloned.1.call-done = bf16[1,768,768]{1,2,0:T(8,128)(2,1)} async-done(((bf16[1,768,192]{1,2,0:T(8,128)(2,1)}), bf16[1,768,768]{1,2,0:T(8,128)(2,1)}) %all-gather.10.cloned.1.call-update) | async-done | bytes 1179664 | tf_op jit(solution)/shard_map/all_gather | solution.py:252
  411.8 3.5 fusion.31
  415.3 29.5 %reduce-scatter.27.cloned.1.call-done = f32[128,768]{1,0:T(8,128)} async-done(((f32[512,768]{1,0:T(8,128)}), f32[128,768]{1,0:T(8,128)}) %reduce-scatter.27.cloned.1.call-update) | async-done | bytes 393232 | tf_op jit(solution)/shard_map/reduce_scatter | solution.py:31
  448.0 31.4 %reduce-scatter.23.cloned.1.call-done = f32[128,768]{1,0:T(8,128)} async-done(((f32[512,768]{1,0:T(8,128)}), f32[128,768]{1,0:T(8,128)}) %reduce-scatter.23.cloned.1.call-update) | async-done | bytes 393232 | tf_op jit(solution)/shard_map/reduce_scatter | solution.py:31
  479.4 2.6 fusion.179
  482.0 11.1 all_gather.60
  493.1 5.3 multiply_convert_fusion.2
  509.2 23.3 %reduce-scatter.29.cloned.1.call-done = f32[128,768]{1,0:T(8,128)} async-done(((f32[512,768]{1,0:T(8,128)}), f32[128,768]{1,0:T(8,128)}) %reduce-scatter.29.cloned.1.call-update) | async-done | bytes 393232 | tf_op jit(solution)/shard_map/reduce_scatter | solution.py:31
  535.7 16.5 %psum.21 = f32[8,768]{1,0:T(8,128)} all-reduce(f32[8,768]{1,0:T(8,128)} %pad_maximum_fusion), channel_id=1, replica_groups=mesh['enc'=2,'dp'=4,'mp'=4] {'mp'}, use_global_device_ids=true, to_apply=%region_22.23 | all-reduce | flops 6144 | bytes 49152 | tf_op jit(solution)/shard_map/psum | solution.py:271
  552.3 24.7 %all_gather.61 = f32[64,768]{1,0:T(8,128)S(1)} all-gather(f32[8,768]{1,0:T(8,128)} %psum.21), channel_id=1, replica_groups=mesh['enc'=2,'dp'=4,'mp'=4] {'enc','dp'}, dimensions={0}, use_global_device_ids=true | all-gather | bytes 221184 | tf_op jit(solution)/shard_map/all_gather | solution.py:272
  605.6 12.2 all_gather.64
  623.6 15.7 %all_gather.62 = bf16[512,768]{1,0:T(8,128)(2,1)S(1)} all-gather(bf16[128,768]{1,0:T(8,128)(2,1)S(1)} %add_convert_fusion.5), channel_id=1, replica_groups=mesh['enc'=2,'dp'=4,'mp'=4] {'mp'}, dimensions={0}, use_global_device_ids=true | all-gather | bytes 983040 | tf_op jit(solution)/shard_map/all_gather | solution.py:27
  639.3 3.3 add_convert_fusion.1
  645.6 8.6 reduce-scatter.35.cloned.1.call-done
  654.1 34.5 %reduce-scatter.31.cloned.1.call-done = f32[128,768]{1,0:T(8,128)} async-done(((f32[512,768]{1,0:T(8,128)}), f32[128,768]{1,0:T(8,128)}) %reduce-scatter.31.cloned.1.call-update) | async-done | bytes 393232 | tf_op jit(solution)/shard_map/reduce_scatter | solution.py:31
  695.6 11.1 all_gather.63
  716.6 14.9 all_gather.65
  739.8 9.0 reduce-scatter.33.cloned.1.call-done
  748.9 34.5 %reduce-scatter.37.cloned.1.call-done = f32[128,768]{1,0:T(8,128)} async-done(((f32[512,768]{1,0:T(8,128)}), f32[128,768]{1,0:T(8,128)}) %reduce-scatter.37.cloned.1.call-update) | async-done | bytes 393232 | tf_op jit(solution)/shard_map/reduce_scatter | solution.py:31
  790.7 4.3 copy.238
  808.1 2.9 copy.258
  811.0 2.8 reshape.1031
  814.5 3.7 all-gather.12.cloned.1.call-done
  819.8 31.7 %all-gather.14.cloned.1.call-done = f32[512,768]{1,0:T(8,128)} async-done(((f32[128,768]{1,0:T(8,128)}), f32[512,768]{1,0:T(8,128)}) %all-gather.14.cloned.1.call-update) | async-done | bytes 1572880 | tf_op jit(solution)/shard_map/all_gather | solution.py:308
  853.1 16.9 %scatter_custom_fusion.1 = f32[7680,768]{1,0:T(8,128)} fusion(s32[1024]{0:T(1024)S(1)} %bitcast.302, f32[]{:T(128)} %constant.335.clone.1, f32[512,768]{1,0:T(8,128)S(1)} %broadcast_select_fusion, f32[]{:T(128)} %constant.342.clone.1, f32[512,768]{1,0:T(8,128)S(1)} %broadcast_select_fusion.1), kind=kCustom, calls=%fused_computation.5 | custom fusion | flops 1572864 | bytes 26738696 | tf_op jit(solution)/shard_map/add | solution.py:317
  875.1 74.9 %all-reduce.3.cloned.1.call-done = f32[1,768,768]{1,0,2:T(1,128)} async-done(((f32[1,768,768]{1,0,2:T(1,128)}), f32[1,768,768]{1,0,2:T(1,128)}) %all-reduce.3.cloned.1.call-update) | async-done | bytes 2359312
  950.0 3.6 multiply_reduce_fusion.3
  953.7 20.8 %reduce-scatter.45.cloned.1.call-done = f32[192,192]{1,0:T(8,128)} async-done(((f32[768,192]{1,0:T(8,128)}), f32[192,192]{1,0:T(8,128)}) %reduce-scatter.45.cloned.1.call-update) | async-done | bytes 147472
  976.3 48.2 %reduce-scatter.41.cloned.1.call-done = f32[1,192,768]{2,1,0:T(8,128)} async-done(((f32[1,768,768]{2,1,0:T(8,128)}), f32[1,192,768]{2,1,0:T(8,128)}) %reduce-scatter.41.cloned.1.call-update) | async-done | bytes 589840 | tf_op jit(solution)/shard_map/reduce_scatter | solution.py:323
  1026.5 77.3 %psum.22 = f32[6,768]{1,0:T(8,128)S(1)} all-reduce(f32[6,768]{1,0:T(8,128)S(1)} %add.660), channel_id=1, replica_groups=mesh['enc'=2,'dp'=4,'mp'=4] {'dp','mp'}, use_global_device_ids=true, to_apply=%region_60.61 | all-reduce | flops 4608 | bytes 36864 | tf_op jit(solution)/shard_map/psum | solution.py:326
  1107.5 352.3 %reduce-scatter.39.cloned.1.call-done = f32[1,1920,768]{2,1,0:T(8,128)} async-done(((f32[1,7680,768]{2,1,0:T(8,128)}), f32[1,1920,768]{2,1,0:T(8,128)}) %reduce-scatter.39.cloned.1.call-update) | async-done | bytes 5898256 | tf_op jit(solution)/shard_map/reduce_scatter | solution.py:320
  1459.8 4.8 multiply_reduce_fusion
  1468.4 42.6 %psum.23 = f32[]{:T(128)} all-reduce(f32[]{:T(128)S(6)} %add.670), channel_id=1, replica_groups=mesh['enc'=2,'dp'=4,'mp'=4] {'enc','dp','mp'}, use_global_device_ids=true, to_apply=%region_77.78 | all-reduce | flops 1 | bytes 8 | tf_op jit(solution)/shard_map/psum | solution.py:331
  1521.5 2.9 multiply_subtract_fusion.1
  1525.9 12.6 multiply_subtract_fusion
  (584 shorter events, 158.7 us)
Async XLA Ops:
  7.2 240.8 %all-gather.6.cloned.1.call-start = ((), (), s32[]{:S(2)}) async-start(), calls=%async_computation.14 | async-start | bytes 14745600 | tf_op jit(solution)/shard_map/all_gather | solution.py:248
  11.8 271.1 %reduce-scatter.19.cloned.1.call-start = ((), (), s32[]{:S(2)}) async-start(), calls=%async_computation.15 | async-start | bytes 983040 | tf_op jit(solution)/shard_map/reduce_scatter | solution.py:76
  64.5 296.3 %copy-start.8 = (bf16[1,768,3,192]{1,3,2,0:T(8,128)(2,1)}, bf16[1,768,3,192]{1,3,2,0:T(8,128)(2,1)S(1)}, u32[]{:S(2)}) copy-start(bf16[1,768,3,192]{1,3,2,0:T(8,128)(2,1)S(1)} %copy.213) | copy-start | bytes 2654212
  97.6 207.4 %copy-start.10 = (bf16[1,192,768]{2,1,0:T(8,128)(2,1)}, bf16[1,192,768]{2,1,0:T(8,128)(2,1)S(1)}, u32[]{:S(2)}) copy-start(bf16[1,192,768]{2,1,0:T(8,128)(2,1)S(1)} %copy.220) | copy-start | bytes 884740
  97.7 158.6 %copy-start.89 = (s32[512,1]{0,1:T(1,128)}, s32[512,1]{0,1:T(1,128)S(1)}, u32[]{:S(2)}) copy-start(s32[512,1]{0,1:T(1,128)S(1)} %get-tuple-element.262) | copy-start | bytes 6148
  97.7 159.8 %copy-start.87 = (s32[512,1]{0,1:T(1,128)}, s32[512,1]{0,1:T(1,128)S(1)}, u32[]{:S(2)}) copy-start(s32[512,1]{0,1:T(1,128)S(1)} %get-tuple-element.261) | copy-start | bytes 6148
  97.7 158.5 %copy-start.126 = (pred[512]{0:T(512)(128)(4,1)}, pred[512]{0:T(512)(128)(4,1)S(1)}, u32[]{:S(2)}) copy-start(pred[512]{0:T(512)(128)(4,1)S(1)} %fusion.142) | copy-start | bytes 1540
  257.4 56.0 %reduce-scatter.25.cloned.1.call-start = ((), (), s32[]{:S(2)}) async-start(), calls=%async_computation.20 | async-start | bytes 983040 | tf_op jit(solution)/shard_map/reduce_scatter | solution.py:76
  258.3 221.1 %copy-start.81 = (f32[768]{0:T(1024)}, f32[768]{0:T(1024)S(1)}, u32[]{:S(2)}) copy-start(f32[768]{0:T(1024)S(1)} %get-tuple-element.139) | copy-start | bytes 9220
  258.3 274.1 %copy-start.75 = (f32[768]{0:T(1024)}, f32[768]{0:T(1024)S(1)}, u32[]{:S(2)}) copy-start(f32[768]{0:T(1024)S(1)} %get-tuple-element.140) | copy-start | bytes 9220
  258.3 276.2 %copy-start.77 = (f32[768]{0:T(1024)}, f32[768]{0:T(1024)S(1)}, u32[]{:S(2)}) copy-start(f32[768]{0:T(1024)S(1)} %get-tuple-element.138) | copy-start | bytes 9220
  268.9 78.8 %reduce-scatter.21.cloned.1.call-start = ((), (), s32[]{:S(2)}) async-start(), calls=%async_computation.16 | async-start | bytes 1966080 | tf_op jit(solution)/shard_map/reduce_scatter | solution.py:31
  306.5 77.1 %all-gather.8.cloned.1.call-start = ((), (), s32[]{:S(2)}) async-start(), calls=%async_computation.17 | async-start | bytes 1474560 | tf_op jit(solution)/shard_map/all_gather | solution.py:251
  308.5 103.3 %all-gather.10.cloned.1.call-start = ((), (), s32[]{:S(2)}) async-start(), calls=%async_computation.18 | async-start | bytes 1474560 | tf_op jit(solution)/shard_map/all_gather | solution.py:252
  309.3 135.5 %reduce-scatter.27.cloned.1.call-start = ((), (), s32[]{:S(2)}) async-start(), calls=%async_computation.21 | async-start | bytes 1966080 | tf_op jit(solution)/shard_map/reduce_scatter | solution.py:31
  314.4 48.8 %copy-start.93 = (f32[128]{0:T(128)}, f32[128]{0:T(128)S(1)}, u32[]{:S(2)}) copy-start(f32[128]{0:T(128)S(1)} %broadcast_multiply_fusion.2) | copy-start | bytes 1540
  316.2 47.1 %copy-start.119 = (f32[128]{0:T(128)}, f32[128]{0:T(128)S(1)}, u32[]{:S(2)}) copy-start(f32[128]{0:T(128)S(1)} %fusion.156) | copy-start | bytes 1540
  370.9 108.5 %reduce-scatter.23.cloned.1.call-start = ((), (), s32[]{:S(2)}) async-start(), calls=%async_computation.19 | async-start | bytes 1966080 | tf_op jit(solution)/shard_map/reduce_scatter | solution.py:31
  415.3 117.2 %reduce-scatter.29.cloned.1.call-start = ((), (), s32[]{:S(2)}) async-start(), calls=%async_computation.22 | async-start | bytes 1966080 | tf_op jit(solution)/shard_map/reduce_scatter | solution.py:31
  501.4 152.8 %reduce-scatter.35.cloned.1.call-start = ((), (), s32[]{:S(2)}) async-start(), calls=%async_computation.25 | async-start | bytes 1966080 | tf_op jit(solution)/shard_map/reduce_scatter | solution.py:31
  533.7 46.5 %copy-start.115 = (f32[128]{0:T(128)}, f32[128]{0:T(128)S(1)}, u32[]{:S(2)}) copy-start(f32[128]{0:T(128)S(1)} %broadcast_multiply_fusion) | copy-start | bytes 1540
  621.9 66.8 %reduce-scatter.31.cloned.1.call-start = ((), (), s32[]{:S(2)}) async-start(), calls=%async_computation.23 | async-start | bytes 1966080 | tf_op jit(solution)/shard_map/reduce_scatter | solution.py:31
  645.5 103.4 %reduce-scatter.33.cloned.1.call-start = ((), (), s32[]{:S(2)}) async-start(), calls=%async_computation.24 | async-start | bytes 1966080 | tf_op jit(solution)/shard_map/reduce_scatter | solution.py:31
  715.8 67.6 %reduce-scatter.37.cloned.1.call-start = ((), (), s32[]{:S(2)}) async-start(), calls=%async_computation.26 | async-start | bytes 1966080 | tf_op jit(solution)/shard_map/reduce_scatter | solution.py:31
  737.7 45.7 %copy-start.6 = (bf16[128,768]{1,0:T(8,128)(2,1)S(1)}, bf16[128,768]{1,0:T(8,128)(2,1)}, u32[]{:S(2)}) copy-start(bf16[128,768]{1,0:T(8,128)(2,1)} %reduce-scatter.19.cloned.1.call-done) | copy-start | bytes 589828
  737.7 45.7 %copy-start.7 = (bf16[128,768]{1,0:T(8,128)(2,1)S(1)}, bf16[128,768]{1,0:T(8,128)(2,1)}, u32[]{:S(2)}) copy-start(bf16[128,768]{1,0:T(8,128)(2,1)} %reduce-scatter.25.cloned.1.call-done) | copy-start | bytes 589828
  737.7 45.7 %copy-start.23 = (f32[128,768]{1,0:T(8,128)S(1)}, f32[128,768]{1,0:T(8,128)}, u32[]{:S(2)}) copy-start(f32[128,768]{1,0:T(8,128)} %copy-done.22) | copy-start | bytes 1179652
  737.7 45.6 %copy-start.92 = (f32[128]{0:T(128)S(1)}, f32[128]{0:T(128)}, u32[]{:S(2)}) copy-start(f32[128]{0:T(128)} %copy-done.91) | copy-start | bytes 1540
  737.7 45.6 %copy-start.94 = (f32[128]{0:T(128)S(1)}, f32[128]{0:T(128)}, u32[]{:S(2)}) copy-start(f32[128]{0:T(128)} %copy-done.93) | copy-start | bytes 1540
  737.7 45.6 %copy-start.134 = (f32[128]{0:T(128)S(1)}, f32[128]{0:T(128)}, u32[]{:S(2)}) copy-start(f32[128]{0:T(128)} %copy-done.133) | copy-start | bytes 1540
  737.8 45.6 %copy-start.136 = (f32[128]{0:T(128)S(1)}, f32[128]{0:T(128)}, u32[]{:S(2)}) copy-start(f32[128]{0:T(128)} %copy-done.135) | copy-start | bytes 1540
  739.8 45.1 %copy-start.118 = (f32[128]{0:T(128)S(1)}, f32[128]{0:T(128)}, u32[]{:S(2)}) copy-start(f32[128]{0:T(128)} %copy-done.117) | copy-start | bytes 1540
  739.8 78.5 %all-gather.12.cloned.1.call-start = ((), (), s32[]{:S(2)}) async-start(), calls=%async_computation.27 | async-start | bytes 1966080 | tf_op jit(solution)/shard_map/all_gather | solution.py:308
  787.1 64.4 %all-gather.14.cloned.1.call-start = ((), (), s32[]{:S(2)}) async-start(), calls=%async_computation.28 | async-start | bytes 1966080 | tf_op jit(solution)/shard_map/all_gather | solution.py:308
  787.7 162.3 %all-reduce.3.cloned.1.call-start = ((), (), s32[]{:S(2)}) async-start(), calls=%async_computation.33 | async-start | bytes 4718592
  795.0 179.4 %reduce-scatter.45.cloned.1.call-start = ((), (), s32[]{:S(2)}) async-start(), calls=%async_computation.32 | async-start | bytes 983040
  799.4 225.1 %reduce-scatter.41.cloned.1.call-start = ((), (), s32[]{:S(2)}) async-start(), calls=%async_computation.30 | async-start | bytes 2949120 | tf_op jit(solution)/shard_map/reduce_scatter | solution.py:323
  803.8 301.3 %reduce-scatter.43.cloned.1.call-start = ((), (), s32[]{:S(2)}) async-start(), calls=%async_computation.31 | async-start | bytes 2457600
  813.8 645.9 %reduce-scatter.39.cloned.1.call-start = ((), (), s32[]{:S(2)}) async-start(), calls=%async_computation.29 | async-start | bytes 29491200 | tf_op jit(solution)/shard_map/reduce_scatter | solution.py:320
  872.1 81.5 %copy-start.101 = (f32[768]{0:T(1024)S(1)}, f32[768]{0:T(1024)}, u32[]{:S(2)}) copy-start(f32[768]{0:T(1024)} %get-tuple-element.219) | copy-start | bytes 9220
  872.1 81.5 %copy-start.100 = (f32[768]{0:T(1024)S(1)}, f32[768]{0:T(1024)}, u32[]{:S(2)}) copy-start(f32[768]{0:T(1024)} %get-tuple-element.217) | copy-start | bytes 9220
  872.1 81.5 %copy-start.99 = (f32[768]{0:T(1024)S(1)}, f32[768]{0:T(1024)}, u32[]{:S(2)}) copy-start(f32[768]{0:T(1024)} %get-tuple-element.126) | copy-start | bytes 9220
  873.7 152.6 %copy-start.105 = (f32[768]{0:T(1024)S(1)}, f32[768]{0:T(1024)}, u32[]{:S(2)}) copy-start(f32[768]{0:T(1024)} %get-tuple-element.147) | copy-start | bytes 9220
  873.7 152.6 %copy-start.104 = (f32[768]{0:T(1024)S(1)}, f32[768]{0:T(1024)}, u32[]{:S(2)}) copy-start(f32[768]{0:T(1024)} %get-tuple-element.146) | copy-start | bytes 9220
  873.7 152.6 %copy-start.103 = (f32[768]{0:T(1024)S(1)}, f32[768]{0:T(1024)}, u32[]{:S(2)}) copy-start(f32[768]{0:T(1024)} %get-tuple-element.129) | copy-start | bytes 9220
  873.8 152.7 %copy-start.102 = (f32[768]{0:T(1024)S(1)}, f32[768]{0:T(1024)}, u32[]{:S(2)}) copy-start(f32[768]{0:T(1024)} %get-tuple-element.132) | copy-start | bytes 9220
  975.7 130.8 %copy-start.45 = (f32[1,192,192]{2,1,0:T(8,128)}, f32[1,192,192]{2,1,0:T(8,128)S(1)}, u32[]{:S(2)}) copy-start(f32[1,192,192]{2,1,0:T(8,128)S(1)} %copy.261) | copy-start | bytes 442372
  1107.5 404.3 %copy-start.86 = (f32[1,6,768]{2,0,1:T(1,128)S(1)}, f32[1,6,768]{2,0,1:T(1,128)}, u32[]{:S(2)}) copy-start(f32[1,6,768]{2,0,1:T(1,128)} %param.46) | copy-start | bytes 55300
  (136 other events, 899.2 us)
Sparse Core Ops, SparseCore 0:
  11.9 235.9 all-gather.5
  257.5 25.3 reduce-scatter.18
  286.4 26.9 reduce-scatter.24
  316.8 30.8 reduce-scatter.20
  349.7 30.4 all-gather.7
  382.2 29.5 all-gather.9
  414.8 30.0 reduce-scatter.26
  448.4 30.9 reduce-scatter.22
  501.5 30.9 reduce-scatter.28
  622.0 32.0 reduce-scatter.34
  657.7 30.8 reduce-scatter.30
  715.9 32.9 reduce-scatter.32
  752.4 30.8 reduce-scatter.36
  787.2 30.9 all-gather.11
  820.5 30.9 all-gather.13
  854.3 95.6 all-reduce.2
  952.1 22.3 reduce-scatter.44
  977.2 47.2 reduce-scatter.40
  1027.4 41.8 reduce-scatter.42
  1071.6 388.1 reduce-scatter.38
where the time goes:
time: 1560 us; the launch traced here: 1550 us
  waiting for transfers between devices  924 us (59%)
  blocking collectives  346 us (22%)
  other arithmetic  109 us (7%)
  local copies, waits for them, and re-layouts  76.5 us (5%)
  matrix products  64.4 us (4%)
  between operations  26.6 us (2%)
    reduce_scatter x1, waiting for transfers between devices, on_device(): lax.psum_scatter(totals[0][None], 'dp', scatter_dimension=1, tiled=True)  352 us
    reduce_scatter x8, waiting for transfers between devices, collect_rows(): return lax.psum_scatter(x, 'mp', scatter_dimension=0, tiled=True)  202 us
    all_gather x1, waiting for transfers between devices, on_device(): lax.all_gather(table.astype(jnp.bfloat16), 'dp', axis=1, tiled=True)  150 us
    all_gather x8, blocking collectives, spread_rows(): return lax.all_gather(x, 'mp', axis=0, tiled=True)  102 us
    unnamed x23, waiting for transfers between devices  96.5 us
    psum x1, blocking collectives, on_device(): g_norms = lax.psum(g_norms, ('dp', 'mp'))  77.3 us
    all_gather x1, blocking collectives, on_device(): lax.all_gather(w_mixed.astype(jnp.bfloat16), 'dp', axis=1, tiled=True)  50.5 us
    reduce_scatter x1, waiting for transfers between devices, on_device(): lax.psum_scatter(totals[3][None], 'dp', scatter_dimension=1, tiled=True)  48.2 us
  transfers between devices with their start and end apart: 20, of which 18 were waited for; matrix products, arithmetic and copies ran while one was open for 8% of the time, Pallas kernels for 0%

commit v1 on v0

--- a/solution.py
+++ b/solution.py
@@ -305,7 +305,14 @@
         )
         g_norms = g_norms + span_norms
         flat_ids = ids_span.reshape(-1)
-        d_rows = lax.all_gather(d_embedded, "mp", axis=0, tiled=True)
+        ring = [d_embedded]
+        for hop in range(3):
+            ring.append(lax.ppermute(ring[-1], "mp", [(dev, (dev + 1) % 4) for dev in range(4)]))
+        d_rows = jnp.roll(
+            jnp.concatenate(ring[::-1], axis=0),
+            (lax.axis_index("mp") + 1) * ring[0].shape[0],
+            axis=0,
+        )
         local_row, owned = vocab_place(flat_ids, weights[0].shape[0])
         g_table = (
             jnp.zeros(weights[0].shape, jnp.float32)

time: 1560 us -> 1490 us (0.955)
  waiting for transfers between devices: 924 us -> 846 us
    unnamed x23 -> x21, waiting for transfers between devices: 96.5 us -> 37.4 us
    ppermute x0 -> x6, waiting for transfers between devices: none -> 45.8 us  [on_device(): lax.ppermute(ring[-1], 'mp', [(dev, (dev + 1) % 4) for dev in range(4)])]
    all_gather x2 -> x0, waiting for transfers between devices: 35.4 us -> none  [on_device(): d_rows = lax.all_gather(d_embedded, 'mp', axis=0, tiled=True)]
    reduce_scatter x8, waiting for transfers between devices: 202 us -> 174 us  [collect_rows(): return lax.psum_scatter(x, 'mp', scatter_dimension=0, tiled=True)]
    unnamed x357 -> x369, local copies, waits for them, and re-layouts: 41.6 us -> 44.1 us
  transfers between devices with their start and end apart: 20 -> 24, of which waited for: 18 -> 21; matrix products, arithmetic and copies ran while one was open for 8% -> 9% of each run, Pallas kernels for 0% -> 0%
where the time goes in v1:
time: 1490 us; the launch traced here: 1480 us
  waiting for transfers between devices  846 us (57%)
  blocking collectives  345 us (23%)
  other arithmetic  112 us (8%)
  local copies, waits for them, and re-layouts  79 us (5%)
  matrix products  63.2 us (4%)
  between operations  26.7 us (2%)
    reduce_scatter x1, waiting for transfers between devices, on_device(): lax.psum_scatter(totals[0][None], 'dp', scatter_dimension=1, tiled=True)  352 us
    reduce_scatter x8, waiting for transfers between devices, collect_rows(): return lax.psum_scatter(x, 'mp', scatter_dimension=0, tiled=True)  174 us
    all_gather x1, waiting for transfers between devices, on_device(): lax.all_gather(table.astype(jnp.bfloat16), 'dp', axis=1, tiled=True)  150 us
    all_gather x8, blocking collectives, spread_rows(): return lax.all_gather(x, 'mp', axis=0, tiled=True)  102 us
    psum x1, blocking collectives, on_device(): g_norms = lax.psum(g_norms, ('dp', 'mp'))  77.2 us
    all_gather x1, blocking collectives, on_device(): lax.all_gather(w_mixed.astype(jnp.bfloat16), 'dp', axis=1, tiled=True)  50.5 us
    reduce_scatter x1, waiting for transfers between devices, on_device(): lax.psum_scatter(totals[3][None], 'dp', scatter_dimension=1, tiled=True)  48.2 us
    ppermute x6, waiting for transfers between devices, on_device(): lax.ppermute(ring[-1], 'mp', [(dev, (dev + 1) % 4) for dev in range(4)])  45.8 us
  transfers between devices with their start and end apart: 24, of which 21 were waited for; matrix products, arithmetic and copies ran while one was open for 9% of the time, Pallas kernels for 0%

profile of v1, /device:TPU:0, one launch (start us, length us, event | category | flops | bytes accessed | tf_op | source)
XLA Modules:
  0.0 1478.8 jit_solution(12203234582590836881)
XLA Ops:
  7.2 4.6 convert_element_type.165
  13.2 50.5 %all_gather.48 = bf16[1,768,3,192]{3,2,0,1:T(4,128)(2,1)S(1)} all-gather(bf16[1,192,3,192]{3,2,0,1:T(4,128)(2,1)S(1)} %copy.212), channel_id=1, replica_groups=mesh['enc'=2,'dp'=4,'mp'=4] {'dp'}, dimensions={1}, use_global_device_ids=true | all-gather | bytes 1105920 | tf_op jit(solution)/shard_map/all_gather | solution.py:249
  65.0 32.1 %all_gather.49 = bf16[1,192,768]{1,0,2:T(2,128)(2,1)S(1)} all-gather(bf16[1,192,192]{1,0,2:T(2,128)(2,1)S(1)} %copy.219), channel_id=1, replica_groups=mesh['enc'=2,'dp'=4,'mp'=4] {'dp'}, dimensions={2}, use_global_device_ids=true | all-gather | bytes 368640 | tf_op jit(solution)/shard_map/all_gather | solution.py:250
  97.7 150.2 %all-gather.4.cloned.1.call-done = bf16[1,7680,768]{2,1,0:T(8,128)(2,1)} async-done(((bf16[1,1920,768]{2,1,0:T(8,128)(2,1)}), bf16[1,7680,768]{2,1,0:T(8,128)(2,1)}) %all-gather.4.cloned.1.call-update) | async-done | bytes 11796496 | tf_op jit(solution)/shard_map/all_gather | solution.py:248
  248.0 8.3 gather_fusion
  259.4 8.4 gather_fusion.1
  268.9 14.0 reduce-scatter.19.cloned.1.call-done
  286.3 14.5 all_gather.47
  309.4 4.0 reduce-scatter.25.cloned.1.call-done
  316.1 31.6 %reduce-scatter.21.cloned.1.call-done = f32[128,768]{1,0:T(8,128)} async-done(((f32[512,768]{1,0:T(8,128)}), f32[128,768]{1,0:T(8,128)}) %reduce-scatter.21.cloned.1.call-update) | async-done | bytes 393232 | tf_op jit(solution)/shard_map/reduce_scatter | solution.py:31
  349.6 11.3 all_gather.53
  372.5 11.2 all_gather.50
  383.7 7.3 multiply_convert_fusion.3
  391.0 20.8 %all-gather.8.cloned.1.call-done = bf16[1,768,768]{1,2,0:T(8,128)(2,1)} async-done(((bf16[1,768,192]{1,2,0:T(8,128)(2,1)}), bf16[1,768,768]{1,2,0:T(8,128)(2,1)}) %all-gather.8.cloned.1.call-update) | async-done | bytes 1179664 | tf_op jit(solution)/shard_map/all_gather | solution.py:252
  411.8 3.5 fusion.47
  415.3 29.5 %reduce-scatter.27.cloned.1.call-done = f32[128,768]{1,0:T(8,128)} async-done(((f32[512,768]{1,0:T(8,128)}), f32[128,768]{1,0:T(8,128)}) %reduce-scatter.27.cloned.1.call-update) | async-done | bytes 393232 | tf_op jit(solution)/shard_map/reduce_scatter | solution.py:31
  448.0 31.4 %reduce-scatter.23.cloned.1.call-done = f32[128,768]{1,0:T(8,128)} async-done(((f32[512,768]{1,0:T(8,128)}), f32[128,768]{1,0:T(8,128)}) %reduce-scatter.23.cloned.1.call-update) | async-done | bytes 393232 | tf_op jit(solution)/shard_map/reduce_scatter | solution.py:31
  482.0 11.1 all_gather.54
  493.1 5.3 multiply_convert_fusion.2
  509.4 23.1 %reduce-scatter.29.cloned.1.call-done = f32[128,768]{1,0:T(8,128)} async-done(((f32[512,768]{1,0:T(8,128)}), f32[128,768]{1,0:T(8,128)}) %reduce-scatter.29.cloned.1.call-update) | async-done | bytes 393232 | tf_op jit(solution)/shard_map/reduce_scatter | solution.py:31
  535.6 16.5 %psum.21 = f32[8,768]{1,0:T(8,128)} all-reduce(f32[8,768]{1,0:T(8,128)} %pad_maximum_fusion), channel_id=1, replica_groups=mesh['enc'=2,'dp'=4,'mp'=4] {'mp'}, use_global_device_ids=true, to_apply=%region_22.23 | all-reduce | flops 6144 | bytes 49152 | tf_op jit(solution)/shard_map/psum | solution.py:271
  552.2 24.8 %all_gather.55 = f32[64,768]{1,0:T(8,128)S(1)} all-gather(f32[8,768]{1,0:T(8,128)} %psum.21), channel_id=1, replica_groups=mesh['enc'=2,'dp'=4,'mp'=4] {'enc','dp'}, dimensions={0}, use_global_device_ids=true | all-gather | bytes 221184 | tf_op jit(solution)/shard_map/all_gather | solution.py:272
  605.9 12.1 all_gather.58
  623.9 15.7 %all_gather.56 = bf16[512,768]{1,0:T(8,128)(2,1)S(1)} all-gather(bf16[128,768]{1,0:T(8,128)(2,1)S(1)} %add_convert_fusion.5), channel_id=1, replica_groups=mesh['enc'=2,'dp'=4,'mp'=4] {'mp'}, dimensions={0}, use_global_device_ids=true | all-gather | bytes 983040 | tf_op jit(solution)/shard_map/all_gather | solution.py:27
  639.6 3.3 add_convert_fusion.1
  645.8 8.6 reduce-scatter.35.cloned.1.call-done
  654.4 34.5 %reduce-scatter.31.cloned.1.call-done = f32[128,768]{1,0:T(8,128)} async-done(((f32[512,768]{1,0:T(8,128)}), f32[128,768]{1,0:T(8,128)}) %reduce-scatter.31.cloned.1.call-update) | async-done | bytes 393232 | tf_op jit(solution)/shard_map/reduce_scatter | solution.py:31
  695.9 11.1 all_gather.57
  716.0 14.9 %all_gather.59 = bf16[512,768]{1,0:T(8,128)(2,1)S(1)} all-gather(bf16[128,768]{1,0:T(8,128)(2,1)S(1)} %add_convert_fusion.2), channel_id=1, replica_groups=mesh['enc'=2,'dp'=4,'mp'=4] {'mp'}, dimensions={0}, use_global_device_ids=true | all-gather | bytes 983040 | tf_op jit(solution)/shard_map/all_gather | solution.py:27
  742.5 4.3 copy.238
  761.5 3.0 copy.258
  767.5 15.1 %reduce-scatter.37.cloned.1.call-done = f32[128,768]{1,0:T(8,128)} async-done(((f32[512,768]{1,0:T(8,128)}), f32[128,768]{1,0:T(8,128)}) %reduce-scatter.37.cloned.1.call-update) | async-done | bytes 393232 | tf_op jit(solution)/shard_map/reduce_scatter | solution.py:31
  788.4 10.0 collective-permute-done
  799.0 7.9 collective-permute-done.3
  807.4 7.9 collective-permute-done.1
  815.8 7.9 collective-permute-done.4
  824.5 7.8 collective-permute-done.2
  835.2 4.3 collective-permute-done.5
  842.5 17.2 %scatter_custom_fusion.1 = f32[7680,768]{1,0:T(8,128)} fusion(s32[1024]{0:T(1024)S(1)} %bitcast.302, f32[]{:T(128)} %constant.353.clone.1, f32[512,768]{1,0:T(8,128)S(1)} %fusion.12, f32[]{:T(128)} %constant.360.clone.1, f32[512,768]{1,0:T(8,128)S(1)} %fusion.20), kind=kCustom, calls=%fused_computation.5 | custom fusion | flops 1572864 | bytes 26738696 | tf_op jit(solution)/shard_map/add | solution.py:324
  864.8 16.3 %all-reduce.3.cloned.1.call-done = f32[1,768,768]{1,0,2:T(1,128)} async-done(((f32[1,768,768]{1,0,2:T(1,128)}), f32[1,768,768]{1,0,2:T(1,128)}) %all-reduce.3.cloned.1.call-update) | async-done | bytes 2359312
  881.1 3.6 multiply_reduce_fusion.3
  884.8 20.8 %reduce-scatter.45.cloned.1.call-done = f32[192,192]{1,0:T(8,128)} async-done(((f32[768,192]{1,0:T(8,128)}), f32[192,192]{1,0:T(8,128)}) %reduce-scatter.45.cloned.1.call-update) | async-done | bytes 147472
  907.4 48.2 %reduce-scatter.41.cloned.1.call-done = f32[1,192,768]{2,1,0:T(8,128)} async-done(((f32[1,768,768]{2,1,0:T(8,128)}), f32[1,192,768]{2,1,0:T(8,128)}) %reduce-scatter.41.cloned.1.call-update) | async-done | bytes 589840 | tf_op jit(solution)/shard_map/reduce_scatter | solution.py:330
  957.6 77.2 %psum.22 = f32[6,768]{1,0:T(8,128)S(1)} all-reduce(f32[6,768]{1,0:T(8,128)S(1)} %add.672), channel_id=1, replica_groups=mesh['enc'=2,'dp'=4,'mp'=4] {'dp','mp'}, use_global_device_ids=true, to_apply=%region_60.61 | all-reduce | flops 4608 | bytes 36864 | tf_op jit(solution)/shard_map/psum | solution.py:333
  1038.6 352.1 %reduce-scatter.39.cloned.1.call-done = f32[1,1920,768]{2,1,0:T(8,128)} async-done(((f32[1,7680,768]{2,1,0:T(8,128)}), f32[1,1920,768]{2,1,0:T(8,128)}) %reduce-scatter.39.cloned.1.call-update) | async-done | bytes 5898256 | tf_op jit(solution)/shard_map/reduce_scatter | solution.py:327
  1390.7 4.8 multiply_reduce_fusion
  1399.4 42.3 %psum.23 = f32[]{:T(128)} all-reduce(f32[]{:T(128)S(6)} %add.683), channel_id=1, replica_groups=mesh['enc'=2,'dp'=4,'mp'=4] {'enc','dp','mp'}, use_global_device_ids=true, to_apply=%region_77.79 | all-reduce | flops 1 | bytes 8 | tf_op jit(solution)/shard_map/psum | solution.py:338
  1456.6 12.6 multiply_subtract_fusion
  (603 shorter events, 174.6 us)
Async XLA Ops:
  7.2 240.8 %all-gather.4.cloned.1.call-start = ((), (), s32[]{:S(2)}) async-start(), calls=%async_computation.14 | async-start | bytes 14745600 | tf_op jit(solution)/shard_map/all_gather | solution.py:248
  11.8 271.1 %reduce-scatter.19.cloned.1.call-start = ((), (), s32[]{:S(2)}) async-start(), calls=%async_computation.15 | async-start | bytes 983040 | tf_op jit(solution)/shard_map/reduce_scatter | solution.py:76
  64.5 296.3 %copy-start.8 = (bf16[1,768,3,192]{1,3,2,0:T(8,128)(2,1)}, bf16[1,768,3,192]{1,3,2,0:T(8,128)(2,1)S(1)}, u32[]{:S(2)}) copy-start(bf16[1,768,3,192]{1,3,2,0:T(8,128)(2,1)S(1)} %copy.213) | copy-start | bytes 2654212
  97.6 207.4 %copy-start.10 = (bf16[1,192,768]{2,1,0:T(8,128)(2,1)}, bf16[1,192,768]{2,1,0:T(8,128)(2,1)S(1)}, u32[]{:S(2)}) copy-start(bf16[1,192,768]{2,1,0:T(8,128)(2,1)S(1)} %copy.220) | copy-start | bytes 884740
  97.7 158.6 %copy-start.94 = (s32[512,1]{0,1:T(1,128)}, s32[512,1]{0,1:T(1,128)S(1)}, u32[]{:S(2)}) copy-start(s32[512,1]{0,1:T(1,128)S(1)} %get-tuple-element.259) | copy-start | bytes 6148
  97.7 159.8 %copy-start.92 = (s32[512,1]{0,1:T(1,128)}, s32[512,1]{0,1:T(1,128)S(1)}, u32[]{:S(2)}) copy-start(s32[512,1]{0,1:T(1,128)S(1)} %get-tuple-element.258) | copy-start | bytes 6148
  97.7 158.5 %copy-start.133 = (pred[512]{0:T(512)(128)(4,1)}, pred[512]{0:T(512)(128)(4,1)S(1)}, u32[]{:S(2)}) copy-start(pred[512]{0:T(512)(128)(4,1)S(1)} %fusion.158) | copy-start | bytes 1540
  257.4 56.0 %reduce-scatter.25.cloned.1.call-start = ((), (), s32[]{:S(2)}) async-start(), calls=%async_computation.20 | async-start | bytes 983040 | tf_op jit(solution)/shard_map/reduce_scatter | solution.py:76
  258.3 221.1 %copy-start.86 = (f32[768]{0:T(1024)}, f32[768]{0:T(1024)S(1)}, u32[]{:S(2)}) copy-start(f32[768]{0:T(1024)S(1)} %get-tuple-element.140) | copy-start | bytes 9220
  258.3 274.1 %copy-start.80 = (f32[768]{0:T(1024)}, f32[768]{0:T(1024)S(1)}, u32[]{:S(2)}) copy-start(f32[768]{0:T(1024)S(1)} %get-tuple-element.141) | copy-start | bytes 9220
  258.3 276.2 %copy-start.82 = (f32[768]{0:T(1024)}, f32[768]{0:T(1024)S(1)}, u32[]{:S(2)}) copy-start(f32[768]{0:T(1024)S(1)} %get-tuple-element.139) | copy-start | bytes 9220
  268.9 78.8 %reduce-scatter.21.cloned.1.call-start = ((), (), s32[]{:S(2)}) async-start(), calls=%async_computation.16 | async-start | bytes 1966080 | tf_op jit(solution)/shard_map/reduce_scatter | solution.py:31
  306.5 41.2 %copy-start.5 = (bf16[128,768]{1,0:T(8,128)(2,1)S(1)}, bf16[128,768]{1,0:T(8,128)(2,1)}, u32[]{:S(2)}) copy-start(bf16[128,768]{1,0:T(8,128)(2,1)} %reduce-scatter.19.cloned.1.call-done) | copy-start | bytes 589828
  306.5 77.2 %all-gather.6.cloned.1.call-start = ((), (), s32[]{:S(2)}) async-start(), calls=%async_computation.17 | async-start | bytes 1474560 | tf_op jit(solution)/shard_map/all_gather | solution.py:251
  308.5 103.3 %all-gather.8.cloned.1.call-start = ((), (), s32[]{:S(2)}) async-start(), calls=%async_computation.18 | async-start | bytes 1474560 | tf_op jit(solution)/shard_map/all_gather | solution.py:252
  309.3 135.5 %reduce-scatter.27.cloned.1.call-start = ((), (), s32[]{:S(2)}) async-start(), calls=%async_computation.21 | async-start | bytes 1966080 | tf_op jit(solution)/shard_map/reduce_scatter | solution.py:31
  314.4 48.8 %copy-start.98 = (f32[128]{0:T(128)}, f32[128]{0:T(128)S(1)}, u32[]{:S(2)}) copy-start(f32[128]{0:T(128)S(1)} %broadcast_multiply_fusion.2) | copy-start | bytes 1540
  316.1 47.2 %copy-start.126 = (f32[128]{0:T(128)}, f32[128]{0:T(128)S(1)}, u32[]{:S(2)}) copy-start(f32[128]{0:T(128)S(1)} %fusion.172) | copy-start | bytes 1540
  370.9 108.5 %reduce-scatter.23.cloned.1.call-start = ((), (), s32[]{:S(2)}) async-start(), calls=%async_computation.19 | async-start | bytes 1966080 | tf_op jit(solution)/shard_map/reduce_scatter | solution.py:31
  415.3 117.2 %reduce-scatter.29.cloned.1.call-start = ((), (), s32[]{:S(2)}) async-start(), calls=%async_computation.22 | async-start | bytes 1966080 | tf_op jit(solution)/shard_map/reduce_scatter | solution.py:31
  501.4 153.0 %reduce-scatter.35.cloned.1.call-start = ((), (), s32[]{:S(2)}) async-start(), calls=%async_computation.25 | async-start | bytes 1966080 | tf_op jit(solution)/shard_map/reduce_scatter | solution.py:31
  533.8 46.5 %copy-start.122 = (f32[128]{0:T(128)}, f32[128]{0:T(128)S(1)}, u32[]{:S(2)}) copy-start(f32[128]{0:T(128)S(1)} %broadcast_multiply_fusion) | copy-start | bytes 1540
  622.1 66.8 %reduce-scatter.31.cloned.1.call-start = ((), (), s32[]{:S(2)}) async-start(), calls=%async_computation.23 | async-start | bytes 1966080 | tf_op jit(solution)/shard_map/reduce_scatter | solution.py:31
  645.7 43.2 %copy-start.81 = (f32[768]{0:T(1024)S(1)}, f32[768]{0:T(1024)}, u32[]{:S(2)}) copy-start(f32[768]{0:T(1024)} %copy-done.80) | copy-start | bytes 9220
  645.7 43.2 %copy-start.114 = (f32[128]{0:T(128)S(1)}, f32[128]{0:T(128)}, u32[]{:S(2)}) copy-start(f32[128]{0:T(128)} %copy-done.113) | copy-start | bytes 1540
  645.8 43.2 %copy-start.116 = (f32[128]{0:T(128)S(1)}, f32[128]{0:T(128)}, u32[]{:S(2)}) copy-start(f32[128]{0:T(128)} %copy-done.115) | copy-start | bytes 1540
  645.8 121.7 %reduce-scatter.33.cloned.1.call-start = ((), (), s32[]{:S(2)}) async-start(), calls=%async_computation.24 | async-start | bytes 1966080 | tf_op jit(solution)/shard_map/reduce_scatter | solution.py:31
  715.6 67.0 %reduce-scatter.37.cloned.1.call-start = ((), (), s32[]{:S(2)}) async-start(), calls=%async_computation.26 | async-start | bytes 1966080 | tf_op jit(solution)/shard_map/reduce_scatter | solution.py:31
  739.0 142.1 %all-reduce.3.cloned.1.call-start = ((), (), s32[]{:S(2)}) async-start(), calls=%async_computation.31 | async-start | bytes 4718592
  746.8 158.7 %reduce-scatter.45.cloned.1.call-start = ((), (), s32[]{:S(2)}) async-start(), calls=%async_computation.30 | async-start | bytes 983040
  752.7 202.9 %reduce-scatter.41.cloned.1.call-start = ((), (), s32[]{:S(2)}) async-start(), calls=%async_computation.28 | async-start | bytes 2949120 | tf_op jit(solution)/shard_map/reduce_scatter | solution.py:330
  757.1 279.0 %reduce-scatter.43.cloned.1.call-start = ((), (), s32[]{:S(2)}) async-start(), calls=%async_computation.29 | async-start | bytes 2457600
  767.4 623.3 %reduce-scatter.39.cloned.1.call-start = ((), (), s32[]{:S(2)}) async-start(), calls=%async_computation.27 | async-start | bytes 29491200 | tf_op jit(solution)/shard_map/reduce_scatter | solution.py:327
  784.2 40.3 %copy-start.93 = (s32[512,1]{0,1:T(1,128)S(1)}, s32[512,1]{0,1:T(1,128)}, u32[]{:S(2)}) copy-start(s32[512,1]{0,1:T(1,128)} %copy-done.92) | copy-start | bytes 6148
  784.2 40.3 %copy-start.95 = (s32[512,1]{0,1:T(1,128)S(1)}, s32[512,1]{0,1:T(1,128)}, u32[]{:S(2)}) copy-start(s32[512,1]{0,1:T(1,128)} %copy-done.94) | copy-start | bytes 6148
  785.5 13.0 collective-permute-start
  787.0 19.9 %collective-permute-start.3 = (f32[128,768]{1,0:T(8,128)S(1)}, f32[128,768]{1,0:T(8,128)S(1)}, u32[]{:S(2)}, u32[]{:S(2)}) collective-permute-start(f32[128,768]{1,0:T(8,128)S(1)} %get-tuple-element.215), channel_id=1, source_target_pairs={{0,1},{1,2},{2,3},{3,0},{4,5},{5,6},{6,7},{7,4},{8,9},{9,10},{10,1... | collective-permute-start | bytes 1179656 | tf_op jit(solution)/shard_map/ppermute | solution.py:310
  798.5 16.9 %collective-permute-start.1 = (f32[128,768]{1,0:T(8,128)S(1)}, f32[128,768]{1,0:T(8,128)S(1)}, u32[]{:S(2)}, u32[]{:S(2)}) collective-permute-start(f32[128,768]{1,0:T(8,128)S(1)} %collective-permute-done), channel_id=1, source_target_pairs={{0,1},{1,2},{2,3},{3,0},{4,5},{5,6},{6,7},{7,4},{8,9},{9,10},{10,1... | collective-permute-start | bytes 1179656 | tf_op jit(solution)/shard_map/ppermute | solution.py:310
  806.9 28.3 %copy-start.73 = (f32[128,768]{1,0:T(8,128)}, f32[128,768]{1,0:T(8,128)S(1)}, u32[]{:S(2)}) copy-start(f32[128,768]{1,0:T(8,128)S(1)} %collective-permute-done.3) | copy-start | bytes 1179652
  806.9 16.9 %collective-permute-start.4 = (f32[128,768]{1,0:T(8,128)S(1)}, f32[128,768]{1,0:T(8,128)S(1)}, u32[]{:S(2)}, u32[]{:S(2)}) collective-permute-start(f32[128,768]{1,0:T(8,128)S(1)} %collective-permute-done.3), channel_id=1, source_target_pairs={{0,1},{1,2},{2,3},{3,0},{4,5},{5,6},{6,7},{7,4},{8,9},{9,10},{10,1... | collective-permute-start | bytes 1179656 | tf_op jit(solution)/shard_map/ppermute | solution.py:310
  815.3 17.0 %collective-permute-start.2 = (f32[128,768]{1,0:T(8,128)S(1)}, f32[128,768]{1,0:T(8,128)}, u32[]{:S(2)}, u32[]{:S(2)}) collective-permute-start(f32[128,768]{1,0:T(8,128)S(1)} %collective-permute-done.1), channel_id=1, source_target_pairs={{0,1},{1,2},{2,3},{3,0},{4,5},{5,6},{6,7},{7,4},{8,9},{9,10},{10,1... | collective-permute-start | bytes 1179656 | tf_op jit(solution)/shard_map/ppermute | solution.py:310
  823.7 15.8 %collective-permute-start.5 = (f32[128,768]{1,0:T(8,128)S(1)}, f32[128,768]{1,0:T(8,128)}, u32[]{:S(2)}, u32[]{:S(2)}) collective-permute-start(f32[128,768]{1,0:T(8,128)S(1)} %collective-permute-done.4), channel_id=1, source_target_pairs={{0,1},{1,2},{2,3},{3,0},{4,5},{5,6},{6,7},{7,4},{8,9},{9,10},{10,1... | collective-permute-start | bytes 1179656 | tf_op jit(solution)/shard_map/ppermute | solution.py:310
  863.4 94.1 %copy-start.111 = (f32[768]{0:T(1024)S(1)}, f32[768]{0:T(1024)}, u32[]{:S(2)}) copy-start(f32[768]{0:T(1024)} %get-tuple-element.148) | copy-start | bytes 9220
  863.4 94.1 %copy-start.110 = (f32[768]{0:T(1024)S(1)}, f32[768]{0:T(1024)}, u32[]{:S(2)}) copy-start(f32[768]{0:T(1024)} %get-tuple-element.147) | copy-start | bytes 9220
  863.4 94.1 %copy-start.109 = (f32[768]{0:T(1024)S(1)}, f32[768]{0:T(1024)}, u32[]{:S(2)}) copy-start(f32[768]{0:T(1024)} %get-tuple-element.130) | copy-start | bytes 9220
  863.4 94.1 %copy-start.108 = (f32[768]{0:T(1024)S(1)}, f32[768]{0:T(1024)}, u32[]{:S(2)}) copy-start(f32[768]{0:T(1024)} %get-tuple-element.133) | copy-start | bytes 9220
  906.8 130.8 %copy-start.46 = (f32[1,192,192]{2,1,0:T(8,128)}, f32[1,192,192]{2,1,0:T(8,128)S(1)}, u32[]{:S(2)}) copy-start(f32[1,192,192]{2,1,0:T(8,128)S(1)} %copy.261) | copy-start | bytes 442372
  1038.6 403.9 %copy-start.91 = (f32[1,6,768]{2,0,1:T(1,128)S(1)}, f32[1,6,768]{2,0,1:T(1,128)}, u32[]{:S(2)}) copy-start(f32[1,6,768]{2,0,1:T(1,128)} %param.48) | copy-start | bytes 55300
  (146 other events, 919.2 us)
Sparse Core Ops, SparseCore 0:
  11.9 235.9 all-gather.3
  257.5 25.3 reduce-scatter.18
  286.4 26.9 reduce-scatter.24
  316.8 30.8 reduce-scatter.20
  349.7 30.4 all-gather.5
  382.2 29.5 all-gather.7
  414.8 30.0 reduce-scatter.26
  448.4 30.9 reduce-scatter.22
  501.5 30.9 reduce-scatter.28
  622.3 32.0 reduce-scatter.34
  658.0 30.8 reduce-scatter.30
  715.7 32.9 reduce-scatter.32
  751.7 30.8 reduce-scatter.36
  785.4 95.6 all-reduce.2
  883.2 22.3 reduce-scatter.44
  908.3 47.2 reduce-scatter.40
  958.4 41.9 reduce-scatter.42
  1002.6 388.0 reduce-scatter.38
